TPU v7x, 256 devices: a whole 4x4x8 slice. The times are simulated.
256 devices in a mesh: dp: 8 (over x_hi, y), fsdp: 16 (over z, core), tensor: 2 (over x_lo).
Axes of the slice: x: 4 (x_hi: 2, x_lo: 2; x = x_hi * 2 + x_lo), y: 4, z: 8, core: 2. Of those that a mesh axis runs over, the one named last changes fastest.
Arguments:
- attn_out: bfloat16 [16384, 2560], P(('dp', 'fsdp')), may hold values from -6 to 6
- cotangent: bfloat16 [16384, 5120], P(('dp', 'fsdp'), 'tensor'), may hold values from -6 to 6
- old_weights: bfloat16 [3, 2048, 4096], P(None, 'tensor', 'fsdp'), may hold values from -0.125 to 0.125
- depth_coef: float32 [2], replicated, may hold values from 0.3 to 1
- depth_pick: int32 [2], replicated, may hold values from 0 to 2
- in_blocks: bfloat16 [20, 2, 128, 128], replicated, may hold values from -0.3125 to 0.3125
- in_cols: int32 [20, 2], replicated, may hold values from 0 to 15, all different within a row
- out_blocks: bfloat16 [40, 2, 128, 128], P('tensor'), may hold values from -0.375 to 0.375
- out_cols: int32 [40, 2], P('tensor'), may hold values from 0 to 31, all different within a row
Outputs:
- grown_out: bfloat16 [16384, 5120], P(('dp', 'fsdp'), 'tensor')
- grad_attn: bfloat16 [16384, 2560], P(('dp', 'fsdp'), 'tensor')
- grad_in_blocks: float32 [20, 2, 128, 128], P('tensor')
- grad_out_blocks: float32 [40, 2, 128, 128], P('tensor')
Inputs may be any that keep to these rules, and one draw needn't show every extreme that they name: `in_cols`: each row names 2 different old head blocks; every old head block is named by some row. `out_cols`: each row names 2 different old width blocks; every old width block is named by some row.
All inputs are finite; a program needn't handle non-finite values.
Results may differ from a plain program's by a relative error of at most 0.0095.
Values may be sent and summed in bfloat16 or wider, within the bound.
No kernel may reach another device: no remote copies, remote signals or barrier semaphores. Data moves between devices by JAX's collectives and lax.ppermute only.
A program may use at most 64 MiB of HBM per device.

v0:
```python
import jax
import jax.numpy as jnp
from jax import lax
from jax.sharding import Mesh
from jax.sharding import PartitionSpec as P

HEAD = 128
D_OLD = 4096
HG_OLD = 16
HG_NEW = 20
DEPTH_K = 2
BO_OLD = 32
PEERS = ("xh", "y", "z")


def gathered_mix(mixed_weight):
    return lax.all_gather(mixed_weight, ("z", "c"), axis=1, tiled=True)


def pair_sum(part):
    other = lax.ppermute(part, "xl", [(0, 1), (1, 0)])
    return (part.astype(jnp.float32) + other.astype(jnp.float32)).astype(jnp.bfloat16)


def token_sum(in_terms, out_terms, scale):
    core = lax.axis_index("c")
    peers = lax.axis_size(PEERS)
    ri, ro = (in_terms.shape[0] // 2, out_terms.shape[0] // 2)

    def half(which):
        a = lax.dynamic_slice_in_dim(in_terms, which * ri, ri, 0).reshape(-1, HEAD)
        b = lax.dynamic_slice_in_dim(out_terms, which * ro, ro, 0).reshape(-1, HEAD)
        return jnp.concatenate([a, b], axis=0)

    swap = [(0, 1), (1, 0)]
    other = lax.ppermute(half(1 - core).astype(jnp.bfloat16), "c", swap)
    mine = (half(core) + other.astype(jnp.float32)).astype(jnp.bfloat16)
    rows = mine.shape[0]
    mine = mine.reshape(peers, rows // peers, HEAD)
    parts = lax.all_to_all(mine, PEERS, 0, 0, tiled=True)
    total = (jnp.sum(parts.astype(jnp.float32), axis=0) * scale).astype(jnp.bfloat16)
    spread = jnp.broadcast_to(total[None], mine.shape)
    full = lax.all_to_all(spread, PEERS, 0, 0, tiled=True).reshape(rows, HEAD)
    theirs = lax.ppermute(full, "c", swap)
    first = jnp.where(core == 0, full, theirs).astype(jnp.float32)
    second = jnp.where(core == 0, theirs, full).astype(jnp.float32)
    cut = ri * in_terms.shape[1] * HEAD
    in_sum = jnp.concatenate([first[:cut], second[:cut]], 0).reshape(in_terms.shape)
    out_sum = jnp.concatenate([first[cut:], second[cut:]], 0).reshape(out_terms.shape)
    return (in_sum, out_sum)


def local(
    attn_out,
    cotangent,
    old_weights,
    depth_coef,
    depth_pick,
    in_blocks,
    in_cols,
    out_blocks,
    out_cols,
):
    highest = lax.Precision.HIGHEST
    tok_rows = attn_out.shape[0]
    tensor_half = lax.axis_index("xl")
    tensor_count = lax.axis_size("xl")
    local_old = old_weights.shape[1]
    local_blocks = local_old // HEAD
    rows_in = HG_NEW // tensor_count
    mixed_weight = jnp.zeros(old_weights.shape[1:], jnp.float32)
    for layer_slot in range(DEPTH_K):
        picked = lax.dynamic_index_in_dim(old_weights, depth_pick[layer_slot], 0, keepdims=False)
        mixed_weight = mixed_weight + depth_coef[layer_slot] * picked.astype(jnp.float32)
    mixed_weight = mixed_weight.astype(jnp.bfloat16)
    attn_blocks = attn_out.reshape(tok_rows, HG_NEW, HEAD)
    products = jnp.einsum(
        "trd,rkde->trke", attn_blocks, in_blocks, preferred_element_type=jnp.float32
    )
    local_cols = tensor_half * local_blocks + jnp.arange(local_blocks, dtype=jnp.int32)
    in_hot = (in_cols[:, :, None] == local_cols[None, None, :]).astype(jnp.float32)
    hidden_local = jnp.einsum("trke,rkc->tce", products, in_hot, precision=highest)
    hidden_local = hidden_local.reshape(tok_rows, local_old).astype(jnp.bfloat16)
    full_mix = gathered_mix(mixed_weight)
    old_part = jnp.dot(hidden_local, full_mix, preferred_element_type=jnp.float32)
    old_out = pair_sum(old_part.astype(jnp.bfloat16))
    old_selected = jnp.take(old_out.reshape(tok_rows, BO_OLD, HEAD), out_cols, axis=1)
    grown_out = jnp.einsum(
        "trkd,rkde->tre", old_selected, out_blocks, preferred_element_type=jnp.float32
    )
    grown_out = grown_out.reshape(tok_rows, -1).astype(jnp.bfloat16)
    cot_blocks = cotangent.reshape(tok_rows, out_blocks.shape[0], HEAD)
    backward_terms = jnp.einsum(
        "tre,rkde->trkd", cot_blocks, out_blocks, preferred_element_type=jnp.float32
    )
    out_hot = (out_cols[:, :, None] == jnp.arange(BO_OLD, dtype=jnp.int32)[None, None, :]).astype(
        jnp.float32
    )
    grad_part = jnp.einsum("trkd,rkc->tcd", backward_terms, out_hot, precision=highest).reshape(
        tok_rows, D_OLD
    )
    old_grad = pair_sum(grad_part.astype(jnp.bfloat16))
    hidden_grad_local = jnp.einsum(
        "to,fo->tf", old_grad, full_mix, preferred_element_type=jnp.float32
    ).astype(jnp.bfloat16)
    hidden_grad = lax.all_gather(hidden_grad_local, "xl", axis=1, tiled=True)
    my_in_blocks = lax.dynamic_slice_in_dim(in_blocks, tensor_half * rows_in, rows_in, 0)
    my_in_cols = lax.dynamic_slice_in_dim(in_cols, tensor_half * rows_in, rows_in, 0)
    grad_selected = jnp.take(hidden_grad.reshape(tok_rows, HG_OLD, HEAD), my_in_cols, axis=1)
    grad_attn = jnp.einsum(
        "trke,rkde->trd", grad_selected, my_in_blocks, preferred_element_type=jnp.float32
    )
    grad_attn = grad_attn.reshape(tok_rows, rows_in * HEAD).astype(jnp.bfloat16)
    my_attn = lax.dynamic_slice_in_dim(attn_blocks, tensor_half * rows_in, rows_in, 1)
    in_terms = jnp.einsum(
        "trd,trke->rkde", my_attn, grad_selected, preferred_element_type=jnp.float32
    )
    out_terms = jnp.einsum(
        "trkd,tre->rkde", old_selected, cot_blocks, preferred_element_type=jnp.float32
    )
    grad_scale = float(tok_rows * lax.axis_size(PEERS) * lax.axis_size("c")) ** (-0.5)
    in_sum, out_sum = token_sum(in_terms, out_terms, grad_scale)
    return (grown_out, grad_attn, in_sum, out_sum)


def solution(mesh):
    fine = Mesh(mesh.devices.reshape(2, 4, 8, 2, 2), ("xh", "y", "z", "c", "xl"))
    tokens = ("xh", "y", "z", "c")
    placed = (
        P(tokens, None),
        P(tokens, "xl"),
        P(None, "xl", ("z", "c")),
        P(),
        P(),
        P(),
        P(),
        P("xl", None, None, None),
        P("xl", None),
    )
    return jax.shard_map(
        local,
        mesh=fine,
        in_specs=placed,
        out_specs=(
            P(tokens, "xl"),
            P(tokens, "xl"),
            P("xl", None, None, None),
            P("xl", None, None, None),
        ),
        check_vma=False,
    )
```

profile of v0, /device:TPU:1, one launch (start us, length us, event | category | flops | bytes accessed | tf_op | source)
XLA Modules:
  0.0 239.7 jit_solution(4200298776029856514)
XLA Ops:
  13.8 3.4 %add_convert_fusion.3 = bf16[1,1024,256]{2,1,0:T(8,128)(2,1)} fusion(bf16[3,1024,256]{2,1,0:T(8,128)(2,1)} %param.11, s32[]{:T(128)S(6)} %select_n.56, f32[]{:T(128)} %bitcast.10, s32[]{:T(128)S(6)} %select_n.55, f32[]{:T(128)} %bitcast.8), kind=kLoop, calls=%fused_computation.34 | loop fusion | flops 1572864 | bytes 1572880 | tf_op jit(solution)/shard_map/convert_element_type | solution.py:75
  17.6 2.0 fusion.57
  19.6 3.6 %copy.46 = f32[20,2,128,128]{2,0,1,3:T(8,128)} copy(f32[20,2,128,128]{3,2,1,0:T(8,128)} %fusion.57) | data formatting | bytes 5242880 | tf_op jit(solution)/shard_map/tre,rkde->trkd/dot_general | solution.py:93
  23.1 3.3 %bitcast_convert_fusion = bf16[32,128,128]{2,0,1:T(8,128)(2,1)S(1)} fusion(f32[20,2,128,128]{2,0,1,3:T(8,128)} %copy.46, s32[20,2]{0,1:T(2,128)S(1)} %copy-done.11), kind=kOutput, calls=%fused_computation.12 | convolution fusion | flops 252183808 | bytes 3670176 | tf_op jit(solution)/shard_map/trkd,rkc->tcd/dot_general | solution.py:99
  27.9 2.0 collective-permute-start.1
  30.7 2.2 copy.26
  32.8 3.6 %fusion.56 = f32[20,2,128,128]{3,2,1,0:T(8,128)} fusion(bf16[20,2,128,128]{3,2,1,0:T(8,128)(2,1)} %param.14, bf16[128,20,128,1]{0,2,3,1:T(8,128)(2,1)} %bitcast.130), kind=kOutput, calls=%fused_computation.79 | convolution fusion | flops 167772160 | bytes 4587520 | tf_op jit(solution)/shard_map/trd,rkde->trke/dot_general | solution.py:77
  36.4 3.6 %copy.40 = f32[20,2,128,128]{2,0,1,3:T(8,128)} copy(f32[20,2,128,128]{3,2,1,0:T(8,128)} %fusion.56) | data formatting | bytes 5242880 | tf_op jit(solution)/shard_map/trd,rkde->trke/dot_general | solution.py:77
  40.0 3.0 %fusion.22 = bf16[8,128,128]{2,0,1:T(8,128)(2,1)S(1)} fusion(f32[20,2,128,128]{2,0,1,3:T(8,128)} %copy.40, s32[20,2]{0,1:T(2,128)S(1)} %copy-done.10, s32[8]{0:T(128)S(1)} %iota_add_fusion), kind=kOutput, calls=%fused_computation.29 | convolution fusion | flops 63045952 | bytes 2883776 | tf_op jit(solution)/shard_map/trke,rkc->tce/dot_general | solution.py:82
  43.0 43.8 %all-gather.3.cloned.1.call-done = bf16[1,1024,4096]{2,1,0:T(8,128)(2,1)} async-done(((bf16[1,1024,256]{2,1,0:T(8,128)(2,1)}), bf16[1,1024,4096]{2,1,0:T(8,128)(2,1)}) %all-gather.3.cloned.1.call-update) | async-done | bytes 8388624 | tf_op jit(solution)/shard_map/all_gather | solution.py:17
  86.8 5.8 %fusion.4 = bf16[128,4096]{1,0:T(8,128)(2,1)} fusion(bf16[1,1024,4096]{2,1,0:T(8,128)(2,1)} %all-gather.3.cloned.1.call-done, bf16[16,8,8,128]{3,2,1,0:T(8,128)(2,1)S(1)} %bitcast.137), kind=kOutput, calls=%fused_computation.6 | convolution fusion | flops 1074266112 | bytes 9699328 | tf_op jit(solution)/shard_map/dot_general | solution.py:85
  92.6 4.1 %fusion.25 = bf16[128,1024]{1,0:T(8,128)(2,1)S(1)} fusion(bf16[1,1024,4096]{2,1,0:T(8,128)(2,1)S(1)} %copy-done.1, bf16[128,4096]{1,0:T(8,128)(2,1)} %collective-permute-done.1, bf16[16,8,32,128]{3,2,1,0:T(8,128)(2,1)S(1)} %bitcast.125), kind=kOutput, calls=%fused_computation.30 | convolution fusion | flops 1075970048 | bytes 10747904 | tf_op jit(solution)/shard_map/to,fo->tf/dot_general | solution.py:103
  96.8 26.1 %all_gather.7 = bf16[128,2048]{1,0:T(8,128)(2,1)S(1)} all-gather(bf16[128,1024]{1,0:T(8,128)(2,1)S(1)} %fusion.25), channel_id=1, replica_groups=mesh['xh'=2,'y'=4,'z'=8,'c'=2,'xl'=2] {'xl'}, dimensions={1}, use_global_device_ids=true | all-gather | bytes 786432 | tf_op jit(solution)/shard_map/all_gather | solution.py:106
  127.1 1.9 copy_bitcast_fusion.1
  129.0 1.8 gather_fusion
  130.8 2.4 %copy.29 = bf16[20,2,128,128]{2,3,1,0:T(8,128)(2,1)} copy(bf16[20,2,128,128]{3,2,1,0:T(8,128)(2,1)} %bitcast.128) | data formatting | bytes 2621440 | tf_op jit(solution)/shard_map/jit(_take)/gather | solution.py:87
  133.2 1.9 fusion.15
  143.0 38.0 %all_to_all.10 = bf16[64,60,128]{2,1,0:T(8,128)(2,1)S(1)} all-to-all(bf16[64,60,128]{2,1,0:T(8,128)(2,1)S(1)} %reshape.90), channel_id=1, replica_groups=mesh['xh'=2,'y'=4,'z'=8,'c'=2,'xl'=2] {'xh','y','z'}, dimensions={0} | all-to-all | bytes 1966080 | tf_op jit(solution)/shard_map/all_to_all | solution.py:40
  181.4 34.7 %all_to_all.11 = bf16[64,60,128]{2,1,0:T(8,128)(2,1)} all-to-all(bf16[64,60,128]{2,1,0:T(8,128)(2,1)S(1)} %broadcast_in_dim.40), channel_id=1, replica_groups=mesh['xh'=2,'y'=4,'z'=8,'c'=2,'xl'=2] {'xh','y','z'}, dimensions={0} | all-to-all | bytes 1966080 | tf_op jit(solution)/shard_map/all_to_all | solution.py:43
  216.2 2.2 reshape.91
  218.4 4.0 %collective-permute-start.3 = (bf16[3840,128]{1,0:T(8,128)(2,1)}, bf16[3840,128]{1,0:T(8,128)(2,1)}, u32[]{:S(2)}, u32[]{:S(2)}) collective-permute-start(bf16[3840,128]{1,0:T(8,128)(2,1)} %reshape.91), channel_id=1, source_target_pairs={{0,2},{2,0},{1,3},{3,1},{4,6},{6,4},{5,7},{7,5},{8,10},{10,8},{9,1... | collective-permute-start | bytes 2949128 | tf_op jit(solution)/shard_map/ppermute | solution.py:44
  222.3 2.2 fusion.21
  224.6 1.9 copy.38
  230.1 1.7 pad_maximum_fusion
  (69 shorter events, 22.5 us)
Async XLA Ops:
  7.2 10.4 %copy-start = (bf16[20,2,128,128]{3,2,1,0:T(8,128)(2,1)S(1)}, bf16[20,2,128,128]{3,2,1,0:T(8,128)(2,1)}, u32[]{:S(2)}) copy-start(bf16[20,2,128,128]{3,2,1,0:T(8,128)(2,1)} %param.16) | copy-start | bytes 3932164
  7.2 10.1 %copy-start.9 = (bf16[128,2560]{1,0:T(8,128)(2,1)S(1)}, bf16[128,2560]{1,0:T(8,128)(2,1)}, u32[]{:S(2)}) copy-start(bf16[128,2560]{1,0:T(8,128)(2,1)} %param.10) | copy-start | bytes 1966084
  7.2 79.6 %all-gather.3.cloned.1.call-start = ((), (), s32[]{:S(2)}) async-start(), calls=%async_computation.2 | async-start | bytes 8912896 | tf_op jit(solution)/shard_map/all_gather | solution.py:17
  19.6 3.6 %copy-start.11 = (s32[20,2]{0,1:T(2,128)S(1)}, s32[20,2]{0,1:T(2,128)}, u32[]{:S(2)}) copy-start(s32[20,2]{0,1:T(2,128)} %param.17) | copy-start | bytes 484
  26.5 3.5 %copy-start.10 = (s32[20,2]{0,1:T(2,128)S(1)}, s32[20,2]{0,1:T(2,128)}, u32[]{:S(2)}) copy-start(s32[20,2]{0,1:T(2,128)} %param.15) | copy-start | bytes 484
  27.9 64.7 %collective-permute-start.1 = (bf16[128,4096]{1,0:T(8,128)(2,1)}, bf16[128,4096]{1,0:T(8,128)(2,1)}, u32[]{:S(2)}, u32[]{:S(2)}) collective-permute-start(bf16[128,4096]{1,0:T(8,128)(2,1)} %bitcast.123), channel_id=1, source_target_pairs={{0,1},{1,0},{2,3},{3,2},{4,5},{5,4},{6,7},{7,6},{8,9},{9,8},{10,11... | collective-permute-start | bytes 3145736 | tf_op jit(solution)/shard_map/ppermute | solution.py:21
  86.8 5.8 %copy-start.1 = (bf16[1,1024,4096]{2,1,0:T(8,128)(2,1)S(1)}, bf16[1,1024,4096]{2,1,0:T(8,128)(2,1)}, u32[]{:S(2)}) copy-start(bf16[1,1024,4096]{2,1,0:T(8,128)(2,1)} %all-gather.3.cloned.1.call-done) | copy-start | bytes 25165828
  92.6 34.5 %collective-permute-start = (bf16[128,4096]{1,0:T(8,128)(2,1)}, bf16[128,4096]{1,0:T(8,128)(2,1)}, u32[]{:S(2)}, u32[]{:S(2)}) collective-permute-start(bf16[128,4096]{1,0:T(8,128)(2,1)} %fusion.4), channel_id=1, source_target_pairs={{0,1},{1,0},{2,3},{3,2},{4,5},{5,4},{6,7},{7,6},{8,9},{9,8},{10,11... | collective-permute-start | bytes 3145736 | tf_op jit(solution)/shard_map/ppermute | solution.py:21
  96.8 27.8 %copy-start.4 = (bf16[128,2560]{0,1:T(8,128)(2,1)S(1)}, bf16[128,2560]{0,1:T(8,128)(2,1)}, u32[]{:S(2)}) copy-start(bf16[128,2560]{0,1:T(8,128)(2,1)} %copy.26) | copy-start | bytes 1966084
  126.0 1.1 copy-start.5
  135.1 1.5 copy-start.2
  136.6 2.2 copy-start.6
  137.7 3.7 %collective-permute-start.2 = (bf16[3840,128]{1,0:T(8,128)(2,1)}, bf16[3840,128]{1,0:T(8,128)(2,1)}, u32[]{:S(2)}, u32[]{:S(2)}) collective-permute-start(bf16[3840,128]{1,0:T(8,128)(2,1)} %pad_maximum_fusion.2), channel_id=1, source_target_pairs={{0,2},{2,0},{1,3},{3,1},{4,6},{6,4},{5,7},{7,5},{8,10},{10,8},{9,1... | collective-permute-start | bytes 2949128 | tf_op jit(solution)/shard_map/ppermute | solution.py:36
  181.4 40.9 %copy-start.8 = (bf16[20,128,128]{2,1,0:T(8,128)(2,1)S(1)}, bf16[20,128,128]{2,1,0:T(8,128)(2,1)}, u32[]{:S(2)}) copy-start(bf16[20,128,128]{2,1,0:T(8,128)(2,1)} %gather_fusion.1) | copy-start | bytes 1966084
  216.2 10.3 %copy-start.3 = (bf16[20,2,128,128]{2,3,1,0:T(8,128)(2,1)S(1)}, bf16[20,2,128,128]{2,3,1,0:T(8,128)(2,1)}, u32[]{:S(2)}) copy-start(bf16[20,2,128,128]{2,3,1,0:T(8,128)(2,1)} %copy.29) | copy-start | bytes 3932164
  218.4 9.8 %collective-permute-start.3 = (bf16[3840,128]{1,0:T(8,128)(2,1)}, bf16[3840,128]{1,0:T(8,128)(2,1)}, u32[]{:S(2)}, u32[]{:S(2)}) collective-permute-start(bf16[3840,128]{1,0:T(8,128)(2,1)} %reshape.91), channel_id=1, source_target_pairs={{0,2},{2,0},{1,3},{3,1},{4,6},{6,4},{5,7},{7,5},{8,10},{10,8},{9,1... | collective-permute-start | bytes 2949128 | tf_op jit(solution)/shard_map/ppermute | solution.py:44
  227.1 1.3 copy-start.7
Sparse Core Ops, SparseCore 0:
  17.4 69.4 all-gather.2
where the time goes:
time: 241 us; the launch traced here: 240 us
  blocking collectives  98.8 us (41%)
  waiting for transfers between devices  44.9 us (19%)
  local copies, waits for them, and re-layouts  30.4 us (13%)
  matrix products  28 us (12%)
  between operations  18.2 us (8%)
  other arithmetic  12.2 us (5%)
  starting transfers between devices  7.18 us (3%)
    all_gather x1, waiting for transfers between devices, gathered_mix(): return lax.all_gather(mixed_weight, ('z', 'c'), axis=1, tiled=True)  43.8 us
    all_to_all x1, blocking collectives, token_sum(): parts = lax.all_to_all(mine, PEERS, 0, 0, tiled=True)  38 us
    all_to_all x1, blocking collectives, token_sum(): full = lax.all_to_all(spread, PEERS, 0, 0, tiled=True).reshape(rows, HEAD)  34.7 us
    all_gather x1, blocking collectives, local(): hidden_grad = lax.all_gather(hidden_grad_local, 'xl', axis=1, tiled=True)  26.1 us
    unnamed x29, local copies, waits for them, and re-layouts  9.58 us
    dot_general x1, matrix products, local(): jnp.dot(hidden_local, full_mix, preferred_element_type=jnp.float32)  5.77 us
  transfers between devices with their start and end apart: 5, of which 2 were waited for; matrix products, arithmetic and copies ran while one was open for 18% of the time, Pallas kernels for 0%

commit v1 on v0

--- a/solution.py
+++ b/solution.py
@@ -13,8 +13,14 @@
 PEERS = ("xh", "y", "z")
 
 
+def close_bench(local_array):
+    m_next = jnp.stack([local_array for _ in range(jax.lax.axis_size(("z", "c")))])
+    state_now = jax.lax.all_to_all(m_next, axis_name=("z", "c"), split_axis=0, concat_axis=0)
+    return jnp.concatenate(state_now, axis=1)
+
+
 def gathered_mix(mixed_weight):
-    return lax.all_gather(mixed_weight, ("z", "c"), axis=1, tiled=True)
+    return close_bench(mixed_weight)
 
 
 def pair_sum(part):

time: 241 us -> 357 us (1.48)
  waiting for transfers between devices: 44.9 us -> 160 us
  between operations: 18.2 us -> 4.8 us
  starting transfers between devices: 7.18 us -> 18.3 us
  local copies, waits for them, and re-layouts: 30.4 us -> 34.8 us
    all_to_all x0 -> x1, waiting for transfers between devices: none -> 159 us  [close_bench(): jax.lax.all_to_all(m_next, axis_name=('z', 'c'), split_axis=0, concat_axi...]
    all_gather x1 -> x0, waiting for transfers between devices: 43.8 us -> none  [gathered_mix(): return lax.all_gather(mixed_weight, ('z', 'c'), axis=1, tiled=True)]
    all_to_all x0 -> x1, starting transfers between devices: none -> 10.1 us  [close_bench(): jax.lax.all_to_all(m_next, axis_name=('z', 'c'), split_axis=0, concat_axi...]
    another operation x3 -> x5, local copies, waits for them, and re-layouts: 0.21 us -> 4.73 us  [the longest x2 4.52 us: close_bench(): jnp.stack([local_array for _ in range(jax.lax.axis_size(('z', 'c')))])]
    unnamed x29 -> x27, local copies, waits for them, and re-layouts: 9.58 us -> 9.54 us
  transfers between devices with their start and end apart: 5 -> 5, of which waited for: 2 -> 2; matrix products, arithmetic and copies ran while one was open for 18% -> 13% of each run, Pallas kernels for 0% -> 0%
where the time goes in v1:
time: 357 us; the launch traced here: 356 us
  waiting for transfers between devices  160 us (45%)
  blocking collectives  96.6 us (27%)
  local copies, waits for them, and re-layouts  34.8 us (10%)
  matrix products  30.6 us (9%)
  starting transfers between devices  18.3 us (5%)
  other arithmetic  11.5 us (3%)
  between operations  4.8 us (1%)
    all_to_all x1, waiting for transfers between devices, close_bench(): jax.lax.all_to_all(m_next, axis_name=('z', 'c'), split_axis=0, concat_axi...  159 us
    all_to_all x1, blocking collectives, token_sum(): parts = lax.all_to_all(mine, PEERS, 0, 0, tiled=True)  38.8 us
    all_to_all x1, blocking collectives, token_sum(): full = lax.all_to_all(spread, PEERS, 0, 0, tiled=True).reshape(rows, HEAD)  34.7 us
    all_gather x1, blocking collectives, local(): hidden_grad = lax.all_gather(hidden_grad_local, 'xl', axis=1, tiled=True)  23.1 us
    all_to_all x1, starting transfers between devices, close_bench(): jax.lax.all_to_all(m_next, axis_name=('z', 'c'), split_axis=0, concat_axi...  10.1 us
    unnamed x27, local copies, waits for them, and re-layouts  9.54 us
    dot_general x1, matrix products, local(): jnp.dot(hidden_local, full_mix, preferred_element_type=jnp.float32)  7.25 us
  transfers between devices with their start and end apart: 5, of which 2 were waited for; matrix products, arithmetic and copies ran while one was open for 13% of the time, Pallas kernels for 0%

profile of v1, /device:TPU:1, one launch (start us, length us, event | category | flops | bytes accessed | tf_op | source)
XLA Modules:
  0.0 356.3 jit_solution(8879445128310491203)
XLA Ops:
  7.2 2.7 fusion.25
  10.1 4.3 %stack.5 = bf16[16,1024,256]{1,2,0:T(8,128)(2,1)} broadcast(bf16[1024,256]{0,1:T(8,128)(2,1)S(1)} %copy.27), dimensions={1,2} | broadcast | bytes 8912896 | tf_op jit(solution)/shard_map/stack | solution.py:17
  14.4 10.1 %all-to-all-start = ((bf16[16,1024,256]{1,2,0:T(8,128)(2,1)}), bf16[16,1024,256]{1,2,0:T(8,128)(2,1)}, u32[]{:S(2)}, u32[]{:S(2)}) async-start(bf16[16,1024,256]{1,2,0:T(8,128)(2,1)} %stack.5), calls=%async_computation | async-start | bytes 16777216 | tf_op jit(solution)/shard_map/all_to_all | solution.py:18
  24.9 2.0 fusion.48
  26.9 3.5 copy.47
  30.4 3.3 bitcast_convert_fusion
  36.7 2.2 copy.26
  38.9 3.5 fusion.47
  42.4 3.5 copy.41
  46.3 3.0 fusion.15
  49.3 158.6 %all-to-all-done = bf16[16,1024,256]{1,2,0:T(8,128)(2,1)} async-done(((bf16[16,1024,256]{1,2,0:T(8,128)(2,1)}), bf16[16,1024,256]{1,2,0:T(8,128)(2,1)}, u32[]{:S(2)}, u32[]{:S(2)}) %all-to-all-start) | async-done | bytes 8388640 | tf_op jit(solution)/shard_map/all_to_all | solution.py:18
  207.9 7.2 %convolution_convert_fusion = bf16[128,4096]{1,0:T(8,128)(2,1)} fusion(bf16[1024,4096]{0,1:T(8,128)(2,1)} %bitcast.14, bf16[16,8,8,128]{3,2,1,0:T(8,128)(2,1)S(1)} %bitcast.137), kind=kOutput, calls=%fused_computation.2 | convolution fusion | flops 1074266112 | bytes 9699328 | tf_op jit(solution)/shard_map/dot_general | solution.py:91
  216.4 5.3 %convolution_convert_fusion.1 = bf16[128,1024]{1,0:T(8,128)(2,1)S(1)} fusion(bf16[1024,4096]{0,1:T(8,128)(2,1)} %bitcast.14, bf16[128,4096]{1,0:T(8,128)(2,1)} %collective-permute-done.1, bf16[16,8,32,128]{3,2,1,0:T(8,128)(2,1)S(1)} %bitcast.123), kind=kOutput, calls=%fused_computation.26 | convolution fusion | flops 1075970048 | bytes 10747904 | tf_op jit(solution)/shard_map/to,fo->tf/dot_general | solution.py:109
  221.7 23.1 %all_gather.3 = bf16[128,2048]{1,0:T(8,128)(2,1)S(1)} all-gather(bf16[128,1024]{1,0:T(8,128)(2,1)S(1)} %convolution_convert_fusion.1), channel_id=1, replica_groups=mesh['xh'=2,'y'=4,'z'=8,'c'=2,'xl'=2] {'xl'}, dimensions={1}, use_global_device_ids=true | all-gather | bytes 786432 | tf_op jit(solution)/shard_map/all_gather | solution.py:112
  249.0 1.9 copy_bitcast_fusion.1
  250.8 1.8 gather_fusion
  252.7 2.4 copy.30
  255.1 1.9 fusion.8
  265.6 38.8 %all_to_all.15 = bf16[64,60,128]{2,1,0:T(8,128)(2,1)S(1)} all-to-all(bf16[64,60,128]{2,1,0:T(8,128)(2,1)S(1)} %reshape.91), channel_id=1, replica_groups=mesh['xh'=2,'y'=4,'z'=8,'c'=2,'xl'=2] {'xh','y','z'}, dimensions={0} | all-to-all | bytes 1966080 | tf_op jit(solution)/shard_map/all_to_all | solution.py:46
  304.8 34.7 %all_to_all.16 = bf16[64,60,128]{2,1,0:T(8,128)(2,1)} all-to-all(bf16[64,60,128]{2,1,0:T(8,128)(2,1)S(1)} %broadcast_in_dim.40), channel_id=1, replica_groups=mesh['xh'=2,'y'=4,'z'=8,'c'=2,'xl'=2] {'xh','y','z'}, dimensions={0} | all-to-all | bytes 1966080 | tf_op jit(solution)/shard_map/all_to_all | solution.py:49
  339.5 2.2 reshape.92
  341.7 4.0 %collective-permute-start.3 = (bf16[3840,128]{1,0:T(8,128)(2,1)}, bf16[3840,128]{1,0:T(8,128)(2,1)}, u32[]{:S(2)}, u32[]{:S(2)}) collective-permute-start(bf16[3840,128]{1,0:T(8,128)(2,1)} %reshape.92), channel_id=1, source_target_pairs={{0,2},{2,0},{1,3},{3,1},{4,6},{6,4},{5,7},{7,5},{8,10},{10,8},{9,1... | collective-permute-start | bytes 2949128 | tf_op jit(solution)/shard_map/ppermute | solution.py:50
  345.7 2.2 fusion.14
  347.9 1.9 copy.39
  (68 shorter events, 27.3 us)
Async XLA Ops:
  0.6 24.2 %copy-start = (bf16[20,2,128,128]{3,2,1,0:T(8,128)(2,1)S(1)}, bf16[20,2,128,128]{3,2,1,0:T(8,128)(2,1)}, u32[]{:S(2)}) copy-start(bf16[20,2,128,128]{3,2,1,0:T(8,128)(2,1)} %param.16) | copy-start | bytes 3932164
  14.4 10.1 %copy-start.8 = (bf16[128,2560]{1,0:T(8,128)(2,1)S(1)}, bf16[128,2560]{1,0:T(8,128)(2,1)}, u32[]{:S(2)}) copy-start(bf16[128,2560]{1,0:T(8,128)(2,1)} %param.10) | copy-start | bytes 1966084
  14.4 193.5 %all-to-all-start = ((bf16[16,1024,256]{1,2,0:T(8,128)(2,1)}), bf16[16,1024,256]{1,2,0:T(8,128)(2,1)}, u32[]{:S(2)}, u32[]{:S(2)}) async-start(bf16[16,1024,256]{1,2,0:T(8,128)(2,1)} %stack.5), calls=%async_computation | async-start | bytes 16777216 | tf_op jit(solution)/shard_map/all_to_all | solution.py:18
  26.9 3.5 copy-start.10
  33.7 2.6 copy-start.9
  35.2 181.2 %collective-permute-start.1 = (bf16[128,4096]{1,0:T(8,128)(2,1)}, bf16[128,4096]{1,0:T(8,128)(2,1)}, u32[]{:S(2)}, u32[]{:S(2)}) collective-permute-start(bf16[128,4096]{1,0:T(8,128)(2,1)} %bitcast.121), channel_id=1, source_target_pairs={{0,1},{1,0},{2,3},{3,2},{4,5},{5,4},{6,7},{7,6},{8,9},{9,8},{10,11... | collective-permute-start | bytes 3145736 | tf_op jit(solution)/shard_map/ppermute | solution.py:27
  215.2 33.8 %collective-permute-start = (bf16[128,4096]{1,0:T(8,128)(2,1)}, bf16[128,4096]{1,0:T(8,128)(2,1)}, u32[]{:S(2)}, u32[]{:S(2)}) collective-permute-start(bf16[128,4096]{1,0:T(8,128)(2,1)} %convolution_convert_fusion), channel_id=1, source_target_pairs={{0,1},{1,0},{2,3},{3,2},{4,5},{5,4},{6,7},{7,6},{8,9},{9,8},{10,11... | collective-permute-start | bytes 3145736 | tf_op jit(solution)/shard_map/ppermute | solution.py:27
  221.7 24.7 %copy-start.3 = (bf16[128,2560]{0,1:T(8,128)(2,1)S(1)}, bf16[128,2560]{0,1:T(8,128)(2,1)}, u32[]{:S(2)}) copy-start(bf16[128,2560]{0,1:T(8,128)(2,1)} %copy.26) | copy-start | bytes 1966084
  247.9 1.1 copy-start.4
  257.0 1.5 copy-start.1
  258.5 3.0 copy-start.5
  259.6 4.4 %collective-permute-start.2 = (bf16[3840,128]{1,0:T(8,128)(2,1)}, bf16[3840,128]{1,0:T(8,128)(2,1)}, u32[]{:S(2)}, u32[]{:S(2)}) collective-permute-start(bf16[3840,128]{1,0:T(8,128)(2,1)} %pad_maximum_fusion.2), channel_id=1, source_target_pairs={{0,2},{2,0},{1,3},{3,1},{4,6},{6,4},{5,7},{7,5},{8,10},{10,8},{9,1... | collective-permute-start | bytes 2949128 | tf_op jit(solution)/shard_map/ppermute | solution.py:42
  304.8 40.9 %copy-start.7 = (bf16[20,128,128]{2,1,0:T(8,128)(2,1)S(1)}, bf16[20,128,128]{2,1,0:T(8,128)(2,1)}, u32[]{:S(2)}) copy-start(bf16[20,128,128]{2,1,0:T(8,128)(2,1)} %gather_fusion.1) | copy-start | bytes 1966084
  339.5 10.3 %copy-start.2 = (bf16[20,2,128,128]{2,3,1,0:T(8,128)(2,1)S(1)}, bf16[20,2,128,128]{2,3,1,0:T(8,128)(2,1)}, u32[]{:S(2)}) copy-start(bf16[20,2,128,128]{2,3,1,0:T(8,128)(2,1)} %copy.30) | copy-start | bytes 3932164
  341.7 9.8 %collective-permute-start.3 = (bf16[3840,128]{1,0:T(8,128)(2,1)}, bf16[3840,128]{1,0:T(8,128)(2,1)}, u32[]{:S(2)}, u32[]{:S(2)}) collective-permute-start(bf16[3840,128]{1,0:T(8,128)(2,1)} %reshape.92), channel_id=1, source_target_pairs={{0,2},{2,0},{1,3},{3,1},{4,6},{6,4},{5,7},{7,5},{8,10},{10,8},{9,1... | collective-permute-start | bytes 2949128 | tf_op jit(solution)/shard_map/ppermute | solution.py:50
  350.4 1.3 copy-start.6
